TPU v7x, 32 devices: a whole 2x2x4 slice. The times are simulated.
32 devices in a mesh: ch: 8 (over y, x, core), grp: 4 (over z).
Axes of the slice: x: 2, y: 2, z: 4, core: 2. Of those that a mesh axis runs over, the one named last changes fastest.
Arguments:
- raw: float32 [512, 4096], P(('ch', 'grp')), may hold values from -128 to 128, as said below
- fir_taps: float32 [129], replicated, may hold values from -4 to 4
- chan_map: int32 [4096], replicated, may hold values from 0 to 4095, each once
- order: int32 [3], replicated, may hold values from 0 to 31, as said below
Outputs:
- correlations: float32 [3, 32, 257, 4096], P(None, None, None, ('ch', 'grp'))
Inputs may be any that keep to these rules, and one draw needn't show every extreme that they name: `order`: 3 distinct device indices; the device with flat index i over ch and grp holds regrouped channels i * 128 to (i + 1) * 128 - 1. `raw`: each time sample and each channel has its own scale.
All inputs are finite; a program needn't handle non-finite values.
Results may differ from a plain program's by a relative error of at most 0.0028.
Values may be sent and summed in bfloat16 or wider, within the bound.
No kernel may reach another device: no remote copies, remote signals or barrier semaphores. Data moves between devices by JAX's collectives and lax.ppermute only.
A program may use at most 128 MiB of HBM per device.

v0:
```python
import math
import jax
import jax.numpy as jnp
from jax import lax
from jax.sharding import PartitionSpec as P

BLK = 512
FIR_HALF = 64
HALF = 128
SB = 32
STEPS = 3
LAGS = 257


def from_root(block, axis, holder):
    block = jnp.where(lax.axis_index(axis) == holder, block, jnp.zeros_like(block))
    return lax.psum(block, axis)


def shifted_rows(vector, count, length, period):
    lead = vector.shape[:-1]
    padded = jnp.pad(vector, [(0, 0)] * len(lead) + [(0, period - vector.shape[-1])])
    spread = jnp.broadcast_to(padded[..., None, :], lead + (count, period))
    flat = spread.reshape(lead + (count * period,))
    cut = flat[..., : count * (period - 1)].reshape(lead + (count, period - 1))
    return cut[..., :length]


def local(raw, fir_taps, chan_map, order):
    columns = jnp.take(raw, chan_map, axis=1)
    mixed = lax.all_to_all(columns, ("ch", "grp"), split_axis=1, concat_axis=0, tiled=True)
    samples, width = mixed.shape
    nblocks = samples // BLK
    starts = jnp.arange(nblocks, dtype=jnp.int32) * BLK
    band = shifted_rows(fir_taps, BLK, BLK + 2 * FIR_HALF, 2 * BLK + 2 * FIR_HALF)
    padded = jnp.pad(mixed, ((FIR_HALF, FIR_HALF), (0, 0)))

    def filter_block(start):
        window = lax.dynamic_slice_in_dim(padded, start, BLK + 2 * FIR_HALF, 0)
        return jnp.dot(band, window, precision=lax.Precision.HIGHEST)

    filtered = lax.map(filter_block, starts).reshape(samples, width)
    power = jnp.mean(filtered * filtered, axis=0)
    whitened = (filtered / jnp.sqrt(power + 1e-06)).astype(jnp.bfloat16)
    own_block = whitened[:, :SB].T
    receivers = jnp.pad(whitened, ((HALF, HALF), (0, 0)))
    results = []
    for step in range(STEPS):
        source = from_root(own_block, ("ch", "grp"), order[step])

        def add_block(total, start):
            piece = lax.dynamic_slice_in_dim(source, start, BLK, 1)
            hankel = shifted_rows(piece, LAGS, BLK + 2 * HALF, BLK + 2 * HALF + 1)
            window = lax.dynamic_slice_in_dim(receivers, start, BLK + 2 * HALF, 0)
            return (
                total
                + jnp.einsum("alj,jr->alr", hankel, window, preferred_element_type=jnp.float32),
                None,
            )

        total, unused = lax.scan(add_block, jnp.zeros((SB, LAGS, width), jnp.float32), starts)
        results.append(total / math.sqrt(samples))
    stacked = jnp.stack(results)
    return stacked


def solution(mesh):
    in_specs = (P(("ch", "grp"), None), P(), P(), P())
    out_specs = P(None, None, None, ("ch", "grp"))
    return jax.shard_map(local, mesh=mesh, in_specs=in_specs, out_specs=out_specs, check_vma=False)
```

profile of v0, /device:TPU:8, one launch (start us, length us, event | category | flops | bytes accessed | tf_op | source)
XLA Modules:
  0.0 358.3 jit_solution(10664348099747867866)
XLA Ops:
  6.5 0.7 and_bitcast_fusion
  7.3 0.7 fusion.9
  8.0 1.5 copy.10
  9.5 14.2 %gather_fusion = f32[4096,16]{1,0:T(8,128)} fusion(f32[16,4096]{0,1:T(8,128)S(1)} %copy.10, s32[4096]{0:T(1024)S(1)} %fusion.9), kind=kCustom, calls=%fused_computation | custom fusion | bytes 540672 | tf_op jit(solution)/shard_map/jit(_take)/gather | solution.py:30
  23.7 2.2 copy.11
  25.9 0.7 broadcast_select_fusion
  26.6 6.0 %all-to-all-start = ((f32[16,32,128]{2,0,1:T(8,128)}), f32[16,32,128]{2,0,1:T(8,128)S(1)}, u32[]{:S(2)}, u32[]{:S(2)}) async-start(f32[16,32,128]{2,0,1:T(8,128)} %broadcast_select_fusion), calls=%async_computation | async-start | bytes 524288 | tf_op jit(solution)/shard_map/all_to_all | solution.py:31
  32.7 0.0 all-reduce.9.cloned.1.call-start
  32.7 1.4 fusion.14
  35.9 0.7 pad.25
  36.6 0.2 broadcast_in_dim.55
  36.8 1.6 reshape.55
  38.3 3.6 %reshape.56 = f32[512,1151]{1,0:T(8,128)S(1)} reshape(f32[589312]{0:T(1024)} %bitcast.36) | data formatting | bytes 4714496 | tf_op jit(solution)/shard_map/reshape | solution.py:25
  42.0 0.2 all-to-all-done
  42.2 1.6 multiply_reduce_fusion
  43.8 0.1 divide_convert_fusion
  43.9 0.6 select_bitcast_fusion.2
  44.5 0.0 all-reduce.9.cloned.1.call-update
  44.6 124.5 %all-reduce.9.cloned.1.call-done = (bf16[32,512]{1,0:T(8,128)(2,1)}, bf16[32,512]{1,0:T(8,128)(2,1)}, bf16[32,512]{1,0:T(8,128)(2,1)}) async-done(((bf16[32,512]{1,0:T(8,128)(2,1)}, bf16[32,512]{1,0:T(8,128)(2,1)}, bf16[32,512]{1,0:T(8,128)(2,1)}), (bf16[32,512]{1,0:T(8,128)(2,1)}, bf16[32,512]{1,0:T(8,128)(2,1)}, bf16[32,512]{1,0:T(8,128)(2,1)})) %all-reduce.9.cloned.1.call-update) | async-done | bytes 98320 | tf_op jit(solution)/shard_map/psum | solution.py:17
  169.1 0.8 pad.30
  169.8 0.8 pad.29
  170.6 0.8 pad.27
  171.4 6.4 %broadcast_in_dim.60 = bf16[32,257,769]{2,1,0:T(8,128)(2,1)} broadcast(bf16[32,769]{1,0:T(8,128)(2,1)S(1)} %pad.27), dimensions={0,2} | broadcast | bytes 12697728 | tf_op jit(solution)/shard_map/while/body/eval_jaxpr/broadcast_in_dim | solution.py:23
  177.8 15.3 %reshape.57 = bf16[32,197633]{1,0:T(8,128)(2,1)} reshape(bf16[32,257,769]{2,1,0:T(8,128)(2,1)} %broadcast_in_dim.60) | data formatting | bytes 25297024 | tf_op jit(solution)/shard_map/while/body/eval_jaxpr/reshape | solution.py:24
  193.1 10.5 %slice.44 = bf16[32,197376]{1,0:T(8,128)(2,1)} slice(bf16[32,197633]{1,0:T(8,128)(2,1)} %reshape.57), slice={[0:32], [0:197376]} | slice | bytes 25264128 | tf_op jit(solution)/shard_map/while/body/eval_jaxpr/slice | solution.py:25
  203.6 12.1 %reshape.58 = bf16[32,257,768]{2,1,0:T(8,128)(2,1)} reshape(bf16[32,197376]{1,0:T(8,128)(2,1)} %slice.44) | data formatting | bytes 25264128 | tf_op jit(solution)/shard_map/while/body/eval_jaxpr/reshape | solution.py:25
  215.7 10.2 %multiply_bitcast_fusion.2 = f32[1,32,257,128]{3,2,1,0:T(8,128)} fusion(bf16[32,257,768]{2,1,0:T(8,128)(2,1)} %reshape.58, bf16[512,128]{0,1:T(8,128)(2,1)S(1)} %divide_convert_fusion), kind=kOutput, calls=%fused_computation.4 | convolution fusion | flops 1617956864 | bytes 16973824 | tf_op jit(solution)/shard_map/while/body/eval_jaxpr/alj,jr->alr/dot_general | solution.py:57
  225.9 6.4 %broadcast_in_dim.61 = bf16[32,257,769]{2,1,0:T(8,128)(2,1)} broadcast(bf16[32,769]{1,0:T(8,128)(2,1)S(1)} %pad.29), dimensions={0,2} | broadcast | bytes 12697728 | tf_op jit(solution)/shard_map/while/body/eval_jaxpr/broadcast_in_dim | solution.py:23
  232.3 15.2 %reshape.59 = bf16[32,197633]{1,0:T(8,128)(2,1)} reshape(bf16[32,257,769]{2,1,0:T(8,128)(2,1)} %broadcast_in_dim.61) | data formatting | bytes 25297024 | tf_op jit(solution)/shard_map/while/body/eval_jaxpr/reshape | solution.py:24
  247.5 10.5 %slice.45 = bf16[32,197376]{1,0:T(8,128)(2,1)} slice(bf16[32,197633]{1,0:T(8,128)(2,1)} %reshape.59), slice={[0:32], [0:197376]} | slice | bytes 25264128 | tf_op jit(solution)/shard_map/while/body/eval_jaxpr/slice | solution.py:25
  258.0 12.1 %reshape.60 = bf16[32,257,768]{2,1,0:T(8,128)(2,1)} reshape(bf16[32,197376]{1,0:T(8,128)(2,1)} %slice.45) | data formatting | bytes 25264128 | tf_op jit(solution)/shard_map/while/body/eval_jaxpr/reshape | solution.py:25
  270.1 10.3 %multiply_bitcast_fusion.1 = f32[1,32,257,128]{3,2,1,0:T(8,128)} fusion(bf16[32,257,768]{2,1,0:T(8,128)(2,1)} %reshape.60, bf16[512,128]{0,1:T(8,128)(2,1)S(1)} %divide_convert_fusion), kind=kOutput, calls=%fused_computation.3 | convolution fusion | flops 1617956864 | bytes 16973824 | tf_op jit(solution)/shard_map/while/body/eval_jaxpr/alj,jr->alr/dot_general | solution.py:57
  280.4 6.4 %broadcast_in_dim.62 = bf16[32,257,769]{2,1,0:T(8,128)(2,1)} broadcast(bf16[32,769]{1,0:T(8,128)(2,1)S(1)} %pad.30), dimensions={0,2} | broadcast | bytes 12697728 | tf_op jit(solution)/shard_map/while/body/eval_jaxpr/broadcast_in_dim | solution.py:23
  286.8 15.2 %reshape.61 = bf16[32,197633]{1,0:T(8,128)(2,1)} reshape(bf16[32,257,769]{2,1,0:T(8,128)(2,1)} %broadcast_in_dim.62) | data formatting | bytes 25297024 | tf_op jit(solution)/shard_map/while/body/eval_jaxpr/reshape | solution.py:24
  302.0 10.5 %slice.46 = bf16[32,197376]{1,0:T(8,128)(2,1)} slice(bf16[32,197633]{1,0:T(8,128)(2,1)} %reshape.61), slice={[0:32], [0:197376]} | slice | bytes 25264128 | tf_op jit(solution)/shard_map/while/body/eval_jaxpr/slice | solution.py:25
  312.4 12.1 %reshape.62 = bf16[32,257,768]{2,1,0:T(8,128)(2,1)} reshape(bf16[32,197376]{1,0:T(8,128)(2,1)} %slice.46) | data formatting | bytes 25264128 | tf_op jit(solution)/shard_map/while/body/eval_jaxpr/reshape | solution.py:25
  324.6 6.7 %multiply_bitcast_fusion = f32[1,32,257,128]{3,2,1,0:T(8,128)S(1)} fusion(bf16[32,257,768]{2,1,0:T(8,128)(2,1)} %reshape.62, bf16[512,128]{0,1:T(8,128)(2,1)S(1)} %divide_convert_fusion), kind=kOutput, calls=%fused_computation.2 | convolution fusion | flops 1617956864 | bytes 16973824 | tf_op jit(solution)/shard_map/while/body/eval_jaxpr/alj,jr->alr/dot_general | solution.py:57
  331.2 8.6 %pad_maximum_fusion = f32[3,32,257,128]{3,2,1,0:T(8,128)} fusion(f32[1,32,257,128]{3,2,1,0:T(8,128)S(1)} %multiply_bitcast_fusion, f32[1,32,257,128]{3,2,1,0:T(8,128)} %multiply_bitcast_fusion.1, f32[1,32,257,128]{3,2,1,0:T(8,128)} %multiply_bitcast_fusion.2), kind=kLoop, calls=%fused_computation.1 | loop fusion | flops 6316032 | bytes 25264128 | tf_op jit(solution)/shard_map/stack | solution.py:63
  339.8 11.6 %copy.15 = f32[3,32,257,128]{3,1,2,0:T(8,128)} copy(f32[3,32,257,128]{3,2,1,0:T(8,128)} %pad_maximum_fusion) | data formatting | bytes 25264128 | tf_op jit(solution)/shard_map/stack | solution.py:63
  (1 shorter events, 0.0 us)
Async XLA Ops:
  26.6 15.6 %all-to-all-start = ((f32[16,32,128]{2,0,1:T(8,128)}), f32[16,32,128]{2,0,1:T(8,128)S(1)}, u32[]{:S(2)}, u32[]{:S(2)}) async-start(f32[16,32,128]{2,0,1:T(8,128)} %broadcast_select_fusion), calls=%async_computation | async-start | bytes 524288 | tf_op jit(solution)/shard_map/all_to_all | solution.py:31
  32.7 136.4 %all-reduce.9.cloned.1.call-start = ((), (), s32[]{:S(2)}) async-start(), calls=%async_computation.1 | async-start | bytes 196608 | tf_op jit(solution)/shard_map/psum | solution.py:17
Sparse Core Ops, SparseCore 0:
  44.7 124.3 all-reduce.8
where the time goes:
time: 360 us; the launch traced here: 358 us
  local copies, waits for them, and re-layouts  172 us (48%)
  waiting for transfers between devices  125 us (35%)
  matrix products  28.8 us (8%)
  between operations  15.3 us (4%)
  other arithmetic  11.5 us (3%)
  starting transfers between devices  6.09 us (2%)
    psum x1, waiting for transfers between devices, from_root(): return lax.psum(block, axis)  125 us
    reshape x4, local copies, waits for them, and re-layouts, shifted_rows(): flat = spread.reshape(lead + (count * period,))  47.2 us
    reshape x4, local copies, waits for them, and re-layouts, shifted_rows(): cut = flat[..., :count * (period - 1)].reshape(lead + (count, period - 1))  40 us
    slice x3, local copies, waits for them, and re-layouts, shifted_rows(): cut = flat[..., :count * (period - 1)].reshape(lead + (count, period - 1))  31.4 us
    dot_general x3, matrix products, add_block(): jnp.einsum('alj,jr->alr', hankel, window, preferred_element_type=jnp.floa...  27.2 us
    broadcast_in_dim x4, local copies, waits for them, and re-layouts, shifted_rows(): spread = jnp.broadcast_to(padded[..., None, :], lead + (count, period))  19.5 us
    gather x2, local copies, waits for them, and re-layouts, local(): columns = jnp.take(raw, chan_map, axis=1)  16.4 us
    another operation x1, local copies, waits for them, and re-layouts, local(): stacked = jnp.stack(results)  11.6 us
  transfers between devices with their start and end apart: 2, of which 2 were waited for; matrix products, arithmetic and copies ran while one was open for 2% of the time, Pallas kernels for 0%

commit v1 on v0

--- a/solution.py
+++ b/solution.py
@@ -14,7 +14,7 @@
 
 def from_root(block, axis, holder):
     block = jnp.where(lax.axis_index(axis) == holder, block, jnp.zeros_like(block))
-    return lax.psum(block, axis)
+    return jnp.sum(lax.all_gather(block, axis), axis=0)
 
 
 def shifted_rows(vector, count, length, period):

time: 360 us -> 402 us (1.12)
  waiting for transfers between devices: 125 us -> 163 us
  other arithmetic: 11.5 us -> 15.7 us
    all_gather x0 -> x3, waiting for transfers between devices: none -> 161 us  [from_root(): return jnp.sum(lax.all_gather(block, axis), axis=0)]
    psum x1 -> x0, waiting for transfers between devices: 125 us -> none  [from_root(): return lax.psum(block, axis)]
    reduce_sum x0 -> x3, other arithmetic: none -> 4.15 us  [from_root(): return jnp.sum(lax.all_gather(block, axis), axis=0)]
  transfers between devices with their start and end apart: 2 -> 4, of which waited for: 2 -> 3; matrix products, arithmetic and copies ran while one was open for 2% -> 3% of each run, Pallas kernels for 0% -> 0%
where the time goes in v1:
time: 402 us; the launch traced here: 398 us
  local copies, waits for them, and re-layouts  170 us (42%)
  waiting for transfers between devices  163 us (41%)
  matrix products  28.8 us (7%)
  other arithmetic  15.7 us (4%)
  between operations  15.2 us (4%)
  starting transfers between devices  6.16 us (2%)
    all_gather x3, waiting for transfers between devices, from_root(): return jnp.sum(lax.all_gather(block, axis), axis=0)  161 us
    reshape x4, local copies, waits for them, and re-layouts, shifted_rows(): flat = spread.reshape(lead + (count * period,))  47.2 us
    reshape x4, local copies, waits for them, and re-layouts, shifted_rows(): cut = flat[..., :count * (period - 1)].reshape(lead + (count, period - 1))  40 us
    slice x3, local copies, waits for them, and re-layouts, shifted_rows(): cut = flat[..., :count * (period - 1)].reshape(lead + (count, period - 1))  31.4 us
    dot_general x3, matrix products, add_block(): jnp.einsum('alj,jr->alr', hankel, window, preferred_element_type=jnp.floa...  27.2 us
    broadcast_in_dim x4, local copies, waits for them, and re-layouts, shifted_rows(): spread = jnp.broadcast_to(padded[..., None, :], lead + (count, period))  19.5 us
    gather x2, local copies, waits for them, and re-layouts, local(): columns = jnp.take(raw, chan_map, axis=1)  16.4 us
    another operation x1, local copies, waits for them, and re-layouts, local(): stacked = jnp.stack(results)  11.6 us
  transfers between devices with their start and end apart: 4, of which 3 were waited for; matrix products, arithmetic and copies ran while one was open for 3% of the time, Pallas kernels for 0%

profile of v1, /device:TPU:8, one launch (start us, length us, event | category | flops | bytes accessed | tf_op | source)
XLA Modules:
  0.0 398.3 jit_solution(10226575311335604316)
XLA Ops:
  6.5 0.7 and_bitcast_fusion
  7.3 0.7 fusion.9
  8.0 1.5 copy.10
  9.5 14.2 %gather_fusion = f32[4096,16]{1,0:T(8,128)} fusion(f32[16,4096]{0,1:T(8,128)S(1)} %copy.10, s32[4096]{0:T(1024)S(1)} %fusion.9), kind=kCustom, calls=%fused_computation | custom fusion | bytes 540672 | tf_op jit(solution)/shard_map/jit(_take)/gather | solution.py:30
  23.7 2.2 copy.11
  25.9 0.7 broadcast_select_fusion
  26.6 6.0 %all-to-all-start = ((f32[16,32,128]{2,0,1:T(8,128)}), f32[16,32,128]{2,0,1:T(8,128)S(1)}, u32[]{:S(2)}, u32[]{:S(2)}) async-start(f32[16,32,128]{2,0,1:T(8,128)} %broadcast_select_fusion), calls=%async_computation | async-start | bytes 524288 | tf_op jit(solution)/shard_map/all_to_all | solution.py:31
  32.7 0.0 all-gather.7.cloned.1.call-start
  32.7 1.4 fusion.14
  36.2 0.7 pad.25
  36.9 0.2 broadcast_in_dim.55
  37.0 1.6 reshape.55
  38.6 3.6 reshape.56
  42.2 0.0 all-to-all-done
  42.2 1.6 multiply_reduce_fusion
  43.8 0.1 divide_convert_fusion
  43.9 0.6 select_bitcast_fusion.2
  44.6 0.0 all-gather.7.cloned.1.call-update
  44.6 0.0 all-gather.9.cloned.1.call-start
  44.7 0.7 all-gather.9.cloned.1.call-update
  45.4 0.0 all-gather.11.cloned.1.call-start
  45.4 0.7 all-gather.11.cloned.1.call-update
  46.1 52.6 %all-gather.7.cloned.1.call-done = bf16[1024,512]{1,0:T(8,128)(2,1)} async-done(((bf16[32,512]{1,0:T(8,128)(2,1)}), bf16[1024,512]{1,0:T(8,128)(2,1)}) %all-gather.7.cloned.1.call-update) | async-done | bytes 1048592 | tf_op jit(solution)/shard_map/all_gather | solution.py:17
  98.7 1.4 reduce_sum.46
  100.1 54.4 %all-gather.9.cloned.1.call-done = bf16[1024,512]{1,0:T(8,128)(2,1)} async-done(((bf16[32,512]{1,0:T(8,128)(2,1)}), bf16[1024,512]{1,0:T(8,128)(2,1)}) %all-gather.9.cloned.1.call-update) | async-done | bytes 1048592 | tf_op jit(solution)/shard_map/all_gather | solution.py:17
  154.4 1.4 reduce_sum.47
  155.8 54.4 %all-gather.11.cloned.1.call-done = bf16[1024,512]{1,0:T(8,128)(2,1)} async-done(((bf16[32,512]{1,0:T(8,128)(2,1)}), bf16[1024,512]{1,0:T(8,128)(2,1)}) %all-gather.11.cloned.1.call-update) | async-done | bytes 1048592 | tf_op jit(solution)/shard_map/all_gather | solution.py:17
  210.2 1.4 reduce_sum.48
  211.6 6.4 %broadcast_in_dim.60 = bf16[32,257,769]{2,1,0:T(8,128)(2,1)} broadcast(bf16[32,769]{1,0:T(8,128)(2,1)S(1)} %pad.27), dimensions={0,2} | broadcast | bytes 12697728 | tf_op jit(solution)/shard_map/while/body/eval_jaxpr/broadcast_in_dim | solution.py:23
  218.1 15.3 %reshape.57 = bf16[32,197633]{1,0:T(8,128)(2,1)} reshape(bf16[32,257,769]{2,1,0:T(8,128)(2,1)} %broadcast_in_dim.60) | data formatting | bytes 25297024 | tf_op jit(solution)/shard_map/while/body/eval_jaxpr/reshape | solution.py:24
  233.3 10.5 %slice.44 = bf16[32,197376]{1,0:T(8,128)(2,1)} slice(bf16[32,197633]{1,0:T(8,128)(2,1)} %reshape.57), slice={[0:32], [0:197376]} | slice | bytes 25264128 | tf_op jit(solution)/shard_map/while/body/eval_jaxpr/slice | solution.py:25
  243.8 12.1 %reshape.58 = bf16[32,257,768]{2,1,0:T(8,128)(2,1)} reshape(bf16[32,197376]{1,0:T(8,128)(2,1)} %slice.44) | data formatting | bytes 25264128 | tf_op jit(solution)/shard_map/while/body/eval_jaxpr/reshape | solution.py:25
  255.9 10.2 %multiply_bitcast_fusion.2 = f32[1,32,257,128]{3,2,1,0:T(8,128)} fusion(bf16[32,257,768]{2,1,0:T(8,128)(2,1)} %reshape.58, bf16[512,128]{0,1:T(8,128)(2,1)S(1)} %divide_convert_fusion), kind=kOutput, calls=%fused_computation.4 | convolution fusion | flops 1617956864 | bytes 16973824 | tf_op jit(solution)/shard_map/while/body/eval_jaxpr/alj,jr->alr/dot_general | solution.py:57
  266.1 6.4 %broadcast_in_dim.61 = bf16[32,257,769]{2,1,0:T(8,128)(2,1)} broadcast(bf16[32,769]{1,0:T(8,128)(2,1)S(1)} %pad.29), dimensions={0,2} | broadcast | bytes 12697728 | tf_op jit(solution)/shard_map/while/body/eval_jaxpr/broadcast_in_dim | solution.py:23
  272.6 15.2 %reshape.59 = bf16[32,197633]{1,0:T(8,128)(2,1)} reshape(bf16[32,257,769]{2,1,0:T(8,128)(2,1)} %broadcast_in_dim.61) | data formatting | bytes 25297024 | tf_op jit(solution)/shard_map/while/body/eval_jaxpr/reshape | solution.py:24
  287.8 10.5 %slice.45 = bf16[32,197376]{1,0:T(8,128)(2,1)} slice(bf16[32,197633]{1,0:T(8,128)(2,1)} %reshape.59), slice={[0:32], [0:197376]} | slice | bytes 25264128 | tf_op jit(solution)/shard_map/while/body/eval_jaxpr/slice | solution.py:25
  298.2 12.1 %reshape.60 = bf16[32,257,768]{2,1,0:T(8,128)(2,1)} reshape(bf16[32,197376]{1,0:T(8,128)(2,1)} %slice.45) | data formatting | bytes 25264128 | tf_op jit(solution)/shard_map/while/body/eval_jaxpr/reshape | solution.py:25
  310.4 10.3 %multiply_bitcast_fusion.1 = f32[1,32,257,128]{3,2,1,0:T(8,128)} fusion(bf16[32,257,768]{2,1,0:T(8,128)(2,1)} %reshape.60, bf16[512,128]{0,1:T(8,128)(2,1)S(1)} %divide_convert_fusion), kind=kOutput, calls=%fused_computation.3 | convolution fusion | flops 1617956864 | bytes 16973824 | tf_op jit(solution)/shard_map/while/body/eval_jaxpr/alj,jr->alr/dot_general | solution.py:57
  320.6 6.4 %broadcast_in_dim.62 = bf16[32,257,769]{2,1,0:T(8,128)(2,1)} broadcast(bf16[32,769]{1,0:T(8,128)(2,1)S(1)} %pad.30), dimensions={0,2} | broadcast | bytes 12697728 | tf_op jit(solution)/shard_map/while/body/eval_jaxpr/broadcast_in_dim | solution.py:23
  327.1 15.2 %reshape.61 = bf16[32,197633]{1,0:T(8,128)(2,1)} reshape(bf16[32,257,769]{2,1,0:T(8,128)(2,1)} %broadcast_in_dim.62) | data formatting | bytes 25297024 | tf_op jit(solution)/shard_map/while/body/eval_jaxpr/reshape | solution.py:24
  342.3 10.5 %slice.46 = bf16[32,197376]{1,0:T(8,128)(2,1)} slice(bf16[32,197633]{1,0:T(8,128)(2,1)} %reshape.61), slice={[0:32], [0:197376]} | slice | bytes 25264128 | tf_op jit(solution)/shard_map/while/body/eval_jaxpr/slice | solution.py:25
  352.7 12.1 %reshape.62 = bf16[32,257,768]{2,1,0:T(8,128)(2,1)} reshape(bf16[32,197376]{1,0:T(8,128)(2,1)} %slice.46) | data formatting | bytes 25264128 | tf_op jit(solution)/shard_map/while/body/eval_jaxpr/reshape | solution.py:25
  364.9 6.7 %multiply_bitcast_fusion = f32[1,32,257,128]{3,2,1,0:T(8,128)S(1)} fusion(bf16[32,257,768]{2,1,0:T(8,128)(2,1)} %reshape.62, bf16[512,128]{0,1:T(8,128)(2,1)S(1)} %divide_convert_fusion), kind=kOutput, calls=%fused_computation.2 | convolution fusion | flops 1617956864 | bytes 16973824 | tf_op jit(solution)/shard_map/while/body/eval_jaxpr/alj,jr->alr/dot_general | solution.py:57
  371.5 8.6 %pad_maximum_fusion = f32[3,32,257,128]{3,2,1,0:T(8,128)} fusion(f32[1,32,257,128]{3,2,1,0:T(8,128)S(1)} %multiply_bitcast_fusion, f32[1,32,257,128]{3,2,1,0:T(8,128)} %multiply_bitcast_fusion.1, f32[1,32,257,128]{3,2,1,0:T(8,128)} %multiply_bitcast_fusion.2), kind=kLoop, calls=%fused_computation.1 | loop fusion | flops 6316032 | bytes 25264128 | tf_op jit(solution)/shard_map/stack | solution.py:63
  380.1 11.6 %copy.15 = f32[3,32,257,128]{3,1,2,0:T(8,128)} copy(f32[3,32,257,128]{3,2,1,0:T(8,128)} %pad_maximum_fusion) | data formatting | bytes 25264128 | tf_op jit(solution)/shard_map/stack | solution.py:63
  (4 shorter events, 0.0 us)
Async XLA Ops:
  26.6 15.6 %all-to-all-start = ((f32[16,32,128]{2,0,1:T(8,128)}), f32[16,32,128]{2,0,1:T(8,128)S(1)}, u32[]{:S(2)}, u32[]{:S(2)}) async-start(f32[16,32,128]{2,0,1:T(8,128)} %broadcast_select_fusion), calls=%async_computation | async-start | bytes 524288 | tf_op jit(solution)/shard_map/all_to_all | solution.py:31
  32.7 66.0 %all-gather.7.cloned.1.call-start = ((), (), s32[]{:S(2)}) async-start(), calls=%async_computation.1 | async-start | bytes 1081344 | tf_op jit(solution)/shard_map/all_gather | solution.py:17
  44.6 109.8 %all-gather.9.cloned.1.call-start = ((), (), s32[]{:S(2)}) async-start(), calls=%async_computation.2 | async-start | bytes 1081344 | tf_op jit(solution)/shard_map/all_gather | solution.py:17
  45.4 164.8 %all-gather.11.cloned.1.call-start = ((), (), s32[]{:S(2)}) async-start(), calls=%async_computation.3 | async-start | bytes 1081344 | tf_op jit(solution)/shard_map/all_gather | solution.py:17
Sparse Core Ops, SparseCore 0:
  44.7 53.9 all-gather.6
  101.7 52.7 all-gather.8
  157.4 52.7 all-gather.10
